TPU v7x, 128 devices: a whole 4x4x4 slice. The times are simulated.
128 devices in a mesh: face: 8 (over y, z_hi), tile: 16 (over x, z_lo, core).
Axes of the slice: x: 4, y: 4, z: 4 (z_hi: 2, z_lo: 2; z = z_hi * 2 + z_lo), core: 2. Of those that a mesh axis runs over, the one named last changes fastest.
Arguments:
- latitude_rows: bfloat16 [512, 4096, 128], P(None, ('face', 'tile')), may hold values from -6 to 6
- tile_order: int32 [512], replicated, may hold values from 0 to 511, each once
- neighbours: int32 [512, 8], P(('face', 'tile')), may hold values from 0 to 511, as said below
- rotations: int32 [512, 8], P(('face', 'tile')), may hold values from 0 to 3
- w_first: bfloat16 [3, 3, 128, 128], replicated, may hold values from -0.1875 to 0.1875
- b_first: float32 [128], replicated, may hold values from -3 to 3
- w_second: bfloat16 [3, 3, 128, 128], replicated, may hold values from -0.1875 to 0.1875
- b_second: float32 [128], replicated, may hold values from -3 to 3
Outputs:
- level_output: bfloat16 [512, 64, 64, 128], P(('face', 'tile'))
Inputs may be any that keep to these rules, and one draw needn't show every extreme that they name: `neighbours`: tiles are held in order, 4 a device, devices ordered face-major. Entry k of a row names a tile held by the device whose face index and tile index differ, counted cyclically, from those of the device that holds the row's tile by (-1,0), (+1,0), (0,-1), (0,+1), (-1,-1), (-1,+1), (+1,-1), (+1,+1) for k = 0 to 7.
All inputs are finite; a program needn't handle non-finite values.
Results may differ from a plain program's by a relative error of at most 0.0033.
Values may be sent and summed in bfloat16 or wider, within the bound.
A program may use at most 64 MiB of HBM per device.

v0:
```python
import jax
import jax.numpy as jnp
import numpy as np
from jax import lax
from jax.sharding import PartitionSpec as P

SIDE = 64


STRIP_TABLE = np.array(
    [
        [1, 2, 0, 3],
        [0, 3, 1, 2],
        [3, 1, 2, 0],
        [2, 0, 3, 1],
        [1, 2, 0, 3],
        [1, 2, 0, 3],
        [0, 3, 1, 2],
        [0, 3, 1, 2],
    ],
    np.int32,
)
FLIP_TABLE = np.array(
    [
        [0, 0, 1, 1],
        [0, 0, 1, 1],
        [0, 1, 1, 0],
        [0, 1, 1, 0],
        [0, 0, 1, 1],
        [0, 0, 1, 1],
        [0, 0, 1, 1],
        [0, 0, 1, 1],
    ],
    np.int32,
)


def padded_2(array, sides, width):
    for axis, dim in sides:
        count, length = (lax.axis_size(axis), array.shape[dim])
        up = [(i, (i + 1) % count) for i in range(count)]
        down = [(j, i) for i, j in up]
        last = lax.slice_in_dim(array, length - width, length, axis=dim)
        first = lax.slice_in_dim(array, 0, width, axis=dim)
        before = lax.ppermute(last, axis, up)
        after = lax.ppermute(first, axis, down)
        array = jnp.concatenate([before, array, after], axis=dim)
    return array


def convolve(padded, weight, bias):
    summed = lax.conv_general_dilated(
        padded,
        weight,
        (1, 1),
        "VALID",
        dimension_numbers=("NHWC", "HWIO", "NHWC"),
        preferred_element_type=jnp.float32,
    )
    return summed + bias


def pad_tiles(centre_tiles, neighbours, rotations):
    tile_count = centre_tiles.shape[0]
    tile_side = centre_tiles.shape[1]
    chan_count = centre_tiles.shape[3]
    local_borders = jnp.stack(
        [
            centre_tiles[:, 0],
            centre_tiles[:, tile_side - 1],
            centre_tiles[:, :, 0],
            centre_tiles[:, :, tile_side - 1],
        ],
        1,
    )
    borders = local_borders[None, None]
    nearby = padded_2(borders, (("face", 0), ("tile", 1)), 1)
    pool = nearby.reshape(9 * tile_count * 4, tile_side, chan_count)
    face_ranks = lax.axis_size("face")
    tile_ranks = lax.axis_size("tile")
    owner = neighbours // tile_count
    local_slot = neighbours % tile_count
    face_step = (owner // tile_ranks - lax.axis_index("face") + 1) % face_ranks
    tile_step = (owner % tile_ranks - lax.axis_index("tile") + 1) % tile_ranks
    matches = rotations[:, :, None] == jnp.arange(4, dtype=jnp.int32)
    strip = jnp.sum(jnp.where(matches, jnp.asarray(STRIP_TABLE)[None], 0), axis=2)
    reverse = jnp.sum(jnp.where(matches, jnp.asarray(FLIP_TABLE)[None], 0), axis=2)
    source = ((face_step * 3 + tile_step) * tile_count + local_slot) * 4 + strip
    lines = jnp.take(pool, source.reshape(-1), axis=0).reshape(tile_count, 8, tile_side, chan_count)
    lines = jnp.where((reverse == 1)[:, :, None, None], lines[:, :, ::-1], lines)
    upper = jnp.concatenate([lines[:, 4, -1:], lines[:, 0], lines[:, 5, :1]], 1)
    lower = jnp.concatenate([lines[:, 6, -1:], lines[:, 1], lines[:, 7, :1]], 1)
    middle = jnp.concatenate([lines[:, 2][:, :, None], centre_tiles, lines[:, 3][:, :, None]], 2)
    return jnp.concatenate([upper[:, None], middle, lower[:, None]], 1)


def shards(latitude_rows, tile_order, neighbours, rotations, w_first, b_first, w_second, b_second):
    ordered = jnp.take(latitude_rows, tile_order, axis=0)
    tile_count = neighbours.shape[0]
    chan_count = ordered.shape[2]
    gathered = lax.all_to_all(ordered, ("face", "tile"), split_axis=0, concat_axis=1, tiled=True)
    nested = gathered.reshape(tile_count, SIDE, SIDE, chan_count)
    first_pad = pad_tiles(nested, neighbours, rotations)
    hidden = jax.nn.gelu(convolve(first_pad, w_first, b_first), approximate=False).astype(
        jnp.bfloat16
    )
    second_pad = pad_tiles(hidden, neighbours, rotations)
    second = convolve(second_pad, w_second, b_second)
    return (nested.astype(jnp.float32) + second).astype(jnp.bfloat16)


def solution(mesh):
    return jax.shard_map(
        shards,
        mesh=mesh,
        in_specs=(
            P(None, ("face", "tile"), None),
            P(),
            P(("face", "tile"), None),
            P(("face", "tile"), None),
            P(),
            P(),
            P(),
            P(),
        ),
        out_specs=P(("face", "tile"), None, None, None),
        check_vma=False,
    )
```

profile of v0, /device:TPU:1, one launch (start us, length us, event | category | flops | bytes accessed | tf_op | source)
XLA Modules:
  0.0 260.2 jit_solution(900804994636350588)
XLA Ops:
  1.4 5.4 %gather_fusion = bf16[512,32,128]{2,1,0:T(8,128)(2,1)} fusion(bf16[512,32,128]{2,1,0:T(8,128)(2,1)} %param.12, s32[1024]{0:T(1024)S(1)} %pad_clamp_fusion.1), kind=kCustom, calls=%fused_computation.2 | custom fusion | bytes 8390656 | tf_op jit(solution)/shard_map/jit(_take)/gather | solution.py:98
  6.8 3.2 %broadcast_select_fusion = bf16[512,32,128]{2,1,0:T(8,128)(2,1)S(1)} fusion(bf16[512,32,128]{2,1,0:T(8,128)(2,1)} %gather_fusion, pred[512]{0:T(512)(128)(4,1)S(1)} %compare_and_fusion.1), kind=kLoop, calls=%fused_computation.41 | loop fusion | flops 2097152 | bytes 8389120 | tf_op jit(solution)/shard_map/jit(_take)/select_n | solution.py:98
  10.1 63.7 %all_to_all.15 = bf16[512,32,128]{2,1,0:T(8,128)(2,1)S(1)} all-to-all(bf16[512,32,128]{2,1,0:T(8,128)(2,1)S(1)} %broadcast_select_fusion), channel_id=1, replica_groups=mesh['face'=8,'tile'=16] {'face','tile'}, dimensions={0} | all-to-all | bytes 8388608 | tf_op jit(solution)/shard_map/all_to_all | solution.py:101
  74.6 2.0 copy-done.2
  76.9 1.2 collective-permute-start.1
  78.2 1.8 collective-permute-start
  80.0 10.6 %collective-permute-done.1 = bf16[1,1,4,4,64,128]{5,4,3,2,1,0:T(8,128)(2,1)S(1)} collective-permute-done((bf16[1,1,4,4,64,128]{5,4,3,2,1,0:T(8,128)(2,1)S(1)}, bf16[1,1,4,4,64,128]{5,4,3,2,1,0:T(8,128)(2,1)S(1)}, u32[]{:S(2)}, u32[]{:S(2)}) %collective-permute-start.1) | collective-permute-done | bytes 262176 | tf_op jit(solution)/shard_map/ppermute | solution.py:46
  90.7 2.3 collective-permute-start.3
  93.0 1.0 collective-permute-start.2
  94.2 17.5 %collective-permute-done.3 = bf16[3,1,4,4,64,128]{5,4,3,2,1,0:T(8,128)(2,1)S(1)} collective-permute-done((bf16[3,1,4,4,64,128]{5,4,3,2,1,0:T(8,128)(2,1)S(1)}, bf16[3,1,4,4,64,128]{5,4,3,2,1,0:T(8,128)(2,1)S(1)}, u32[]{:S(2)}, u32[]{:S(2)}) %collective-permute-start.3) | collective-permute-done | bytes 786464 | tf_op jit(solution)/shard_map/ppermute | solution.py:46
  111.7 0.9 copy-done.4
  112.6 1.5 pad_maximum_fusion
  115.6 5.1 %maximum_bitcast_fusion = bf16[66,4,66,128]{3,2,0,1:T(8,128)(2,1)S(1)} fusion(bf16[4,1,66,128]{3,2,1,0:T(8,128)(2,1)S(1)} %maximum_bitcast_fusion.5, bf16[4,64,1,128]{3,2,1,0:T(2,128)(2,1)S(1)} %copy.157, bf16[4,64,64,128]{3,2,1,0:T(8,128)(2,1)} %bitcast.102, bf16[4,64,1,128]{3,2,1,0:T(2,128)(2,1)S(1)} %copy.156, ...), kind=kLoop, calls=%fused_computation.38 | loop fusion | flops 22302720 | bytes 8921088 | tf_op jit(solution)/shard_map/concatenate | solution.py:94
  120.8 1.8 copy.187
  122.6 1.7 pad.clone
  124.7 2.7 %fusion.15 = bf16[66,4,8,11,128]{4,1,3,2,0:T(4,128)(2,1)S(1)} fusion(bf16[66,4,7,2,128]{4,1,3,2,0:T(4,128)(2,1)S(1)} %slice.122, bf16[66,4,8,9,128]{4,1,3,2,0:T(4,128)(2,1)S(1)} %bitcast.108), kind=kLoop, calls=%fused_computation.30 | loop fusion | flops 17842176 | bytes 11759616 | tf_op jit(solution)/shard_map/conv_general_dilated | solution.py:52
  127.4 32.5 %fusion.4 = bf16[64,32,9,128]{3,1,2,0:T(8,128)(2,1)S(1)} fusion(f32[128]{0:T(128)S(1)} %copy-done.10, pred[32,9]{0,1:T(8,128)(4,1)S(1)} %copy-done.12, bf16[3,3,128,128]{3,2,1,0:T(8,128)(2,1)S(1)} %copy-done, bf16[66,4,8,11,128]{4,1,3,2,0:T(4,128)(2,1)S(1)} %fusion.15), kind=kOutput, calls=%fused_computation.9 | convolution fusion | flops 5593890816 | bytes 10961696 | tf_op jit(solution)/shard_map/conv_general_dilated | solution.py:52
  159.9 1.8 copy.166
  161.7 2.9 %copy_bitcast_fusion.1 = bf16[4,64,64,128]{3,1,0,2:T(8,128)(2,1)} fusion(bf16[64,4,72,128]{3,0,2,1:T(8,128)(2,1)S(1)} %bitcast.109), kind=kLoop, calls=%fused_computation.40 | loop fusion | bytes 8388608 | tf_op jit(solution)/shard_map/convert_element_type | solution.py:104
  164.9 0.9 slice_bitcast_fusion.5
  165.8 4.0 %collective-permute-start.5 = (bf16[1,1,4,4,64,128]{5,4,2,3,1,0:T(8,128)(2,1)S(1)}, bf16[1,1,4,4,64,128]{5,4,2,3,1,0:T(8,128)(2,1)S(1)}, u32[]{:S(2)}, u32[]{:S(2)}) collective-permute-start(bf16[1,1,4,4,64,128]{5,4,2,3,1,0:T(8,128)(2,1)S(1)} %maximum_bitcast_fusion.3), channel_id=1, source_target_pairs={{16,0},{32,16},{48,32},{64,48},{80,64},{96,80},{112,96},{0,112},{1... | collective-permute-start | bytes 786440 | tf_op jit(solution)/shard_map/ppermute | solution.py:46
  169.8 16.8 %collective-permute-done.5 = bf16[1,1,4,4,64,128]{5,4,2,3,1,0:T(8,128)(2,1)S(1)} collective-permute-done((bf16[1,1,4,4,64,128]{5,4,2,3,1,0:T(8,128)(2,1)S(1)}, bf16[1,1,4,4,64,128]{5,4,2,3,1,0:T(8,128)(2,1)S(1)}, u32[]{:S(2)}, u32[]{:S(2)}) %collective-permute-start.5) | collective-permute-done | bytes 262176 | tf_op jit(solution)/shard_map/ppermute | solution.py:46
  186.8 1.7 collective-permute-start.6
  188.6 17.7 %collective-permute-done.7 = bf16[3,1,4,4,64,128]{5,4,2,3,1,0:T(8,128)(2,1)S(1)} collective-permute-done((bf16[3,1,4,4,64,128]{5,4,2,3,1,0:T(8,128)(2,1)S(1)}, bf16[3,1,4,4,64,128]{5,4,2,3,1,0:T(8,128)(2,1)S(1)}, u32[]{:S(2)}, u32[]{:S(2)}) %collective-permute-start.7) | collective-permute-done | bytes 786464 | tf_op jit(solution)/shard_map/ppermute | solution.py:46
  208.7 6.6 %maximum_bitcast_fusion.1 = bf16[66,4,66,128]{3,0,1,2:T(8,128)(2,1)S(1)} fusion(bf16[4,1,66,128]{3,1,0,2:T(2,128)(2,1)S(1)} %copy.176, bf16[4,64,1,128]{3,1,0,2:T(8,128)(2,1)S(1)} %get-tuple-element.22, bf16[4,64,64,128]{3,1,0,2:T(8,128)(2,1)} %copy_bitcast_fusion.1, bf16[4,64,1,128]{3,1,0,2:T(8,128)(2,1)S(1)} %get-tuple-element.23, ...), kind=kLoop, calls=%fused_computation.39 | loop fusion | flops 22302720 | bytes 8921088 | tf_op jit(solution)/shard_map/concatenate | solution.py:94
  215.3 1.7 copy.188
  217.1 1.7 pad.2.clone
  219.1 2.7 %fusion.16 = bf16[66,4,8,11,128]{4,1,3,2,0:T(4,128)(2,1)S(1)} fusion(bf16[66,4,7,2,128]{4,1,3,2,0:T(4,128)(2,1)S(1)} %slice.138, bf16[66,4,8,9,128]{4,1,3,2,0:T(4,128)(2,1)S(1)} %bitcast.106), kind=kLoop, calls=%fused_computation.31 | loop fusion | flops 17842176 | bytes 11759616 | tf_op jit(solution)/shard_map/conv_general_dilated | solution.py:52
  221.9 13.9 %select_add_fusion = f32[64,32,9,128]{3,1,2,0:T(8,128)} fusion(f32[128]{0:T(128)S(1)} %copy-done.11, pred[32,9]{0,1:T(8,128)(4,1)S(1)} %copy-done.12, bf16[3,3,128,128]{3,2,1,0:T(8,128)(2,1)S(1)} %copy-done.9, bf16[66,4,8,11,128]{4,1,3,2,0:T(4,128)(2,1)S(1)} %fusion.16), kind=kOutput, calls=%fused_computation.10 | convolution fusion | flops 5440536576 | bytes 15680288 | tf_op jit(solution)/shard_map/conv_general_dilated | solution.py:52
  235.8 9.1 %copy.179 = f32[64,32,9,128]{3,0,2,1:T(8,128)S(1)} copy(f32[64,32,9,128]{3,1,2,0:T(8,128)} %select_add_fusion) | data formatting | bytes 18874368 | tf_op jit(solution)/shard_map/add | solution.py:60
  245.0 4.2 %slice.139 = f32[64,4,64,128]{3,0,2,1:T(8,128)} slice(f32[64,4,72,128]{3,0,2,1:T(8,128)S(1)} %bitcast.104), slice={[0:64], [0:4], [0:64], [0:128]} | slice | bytes 16777216 | tf_op jit(solution)/shard_map/add | solution.py:60
  249.2 10.8 %fusion.14 = bf16[4,64,64,128]{3,2,1,0:T(8,128)(2,1)} fusion(f32[64,4,64,128]{3,0,2,1:T(8,128)} %slice.139, bf16[4,64,64,128]{3,2,1,0:T(8,128)(2,1)S(1)} %bitcast.103), kind=kLoop, calls=%fused_computation.29 | loop fusion | flops 6291456 | bytes 16777216 | tf_op jit(solution)/shard_map/convert_element_type | solution.py:109
  (82 shorter events, 7.9 us)
Async XLA Ops:
  0.0 127.4 %copy-start = (bf16[3,3,128,128]{3,2,1,0:T(8,128)(2,1)S(1)}, bf16[3,3,128,128]{3,2,1,0:T(8,128)(2,1)}, u32[]{:S(2)}) copy-start(bf16[3,3,128,128]{3,2,1,0:T(8,128)(2,1)} %param.16) | copy-start | bytes 884740
  10.1 69.9 %copy-start.5 = (s32[4,8]{1,0:T(4,128)S(1)}, s32[4,8]{1,0:T(4,128)}, u32[]{:S(2)}) copy-start(s32[4,8]{1,0:T(4,128)} %param.15) | copy-start | bytes 388
  10.1 69.8 %copy-start.7 = (s32[8,4]{0,1:T(4,128)S(1)}, s32[8,4]{0,1:T(4,128)}, u32[]{:S(2)}) copy-start(s32[8,4]{0,1:T(4,128)} %constant.182.clone) | copy-start | bytes 388
  10.1 69.8 %copy-start.8 = (s32[8,4]{0,1:T(4,128)S(1)}, s32[8,4]{0,1:T(4,128)}, u32[]{:S(2)}) copy-start(s32[8,4]{0,1:T(4,128)} %constant.181.clone) | copy-start | bytes 388
  10.1 83.9 %copy-start.6 = (s32[4,8]{1,0:T(4,128)S(1)}, s32[4,8]{1,0:T(4,128)}, u32[]{:S(2)}) copy-start(s32[4,8]{1,0:T(4,128)} %param.14) | copy-start | bytes 388
  74.6 2.0 copy-start.2
  76.9 13.7 %collective-permute-start.1 = (bf16[1,1,4,4,64,128]{5,4,3,2,1,0:T(8,128)(2,1)S(1)}, bf16[1,1,4,4,64,128]{5,4,3,2,1,0:T(8,128)(2,1)S(1)}, u32[]{:S(2)}, u32[]{:S(2)}) collective-permute-start(bf16[1,1,4,4,64,128]{5,4,3,2,1,0:T(8,128)(2,1)S(1)} %maximum_bitcast_fusion.2), channel_id=1, source_target_pairs={{16,0},{32,16},{48,32},{64,48},{80,64},{96,80},{112,96},{0,112},{1... | collective-permute-start | bytes 786440 | tf_op jit(solution)/shard_map/ppermute | solution.py:46
  78.2 12.5 %collective-permute-start = (bf16[1,1,4,4,64,128]{5,4,3,2,1,0:T(8,128)(2,1)S(1)}, bf16[1,1,4,4,64,128]{5,4,3,2,1,0:T(8,128)(2,1)S(1)}, u32[]{:S(2)}, u32[]{:S(2)}) collective-permute-start(bf16[1,1,4,4,64,128]{5,4,3,2,1,0:T(8,128)(2,1)S(1)} %maximum_bitcast_fusion.2), channel_id=1, source_target_pairs={{0,16},{16,32},{32,48},{48,64},{64,80},{80,96},{96,112},{112,0},{1... | collective-permute-start | bytes 786440 | tf_op jit(solution)/shard_map/ppermute | solution.py:45
  90.7 21.0 %collective-permute-start.3 = (bf16[3,1,4,4,64,128]{5,4,3,2,1,0:T(8,128)(2,1)S(1)}, bf16[3,1,4,4,64,128]{5,4,3,2,1,0:T(8,128)(2,1)S(1)}, u32[]{:S(2)}, u32[]{:S(2)}) collective-permute-start(bf16[3,1,4,4,64,128]{5,4,3,2,1,0:T(8,128)(2,1)S(1)} %pad_maximum_fusion.2), channel_id=1, source_target_pairs={{1,0},{2,1},{3,2},{4,3},{5,4},{6,5},{7,6},{8,7},{9,8},{10,9},{11,1... | collective-permute-start | bytes 2359304 | tf_op jit(solution)/shard_map/ppermute | solution.py:46
  93.0 19.6 %collective-permute-start.2 = (bf16[3,1,4,4,64,128]{5,4,3,2,1,0:T(8,128)(2,1)S(1)}, bf16[3,1,4,4,64,128]{5,4,3,2,1,0:T(8,128)(2,1)}, u32[]{:S(2)}, u32[]{:S(2)}) collective-permute-start(bf16[3,1,4,4,64,128]{5,4,3,2,1,0:T(8,128)(2,1)S(1)} %pad_maximum_fusion.2), channel_id=1, source_target_pairs={{0,1},{1,2},{2,3},{3,4},{4,5},{5,6},{6,7},{7,8},{8,9},{9,10},{10,1... | collective-permute-start | bytes 2359304 | tf_op jit(solution)/shard_map/ppermute | solution.py:45
  111.7 0.9 copy-start.4
  122.6 4.9 %copy-start.10 = (f32[128]{0:T(128)S(1)}, f32[128]{0:T(128)}, u32[]{:S(2)}) copy-start(f32[128]{0:T(128)} %param.17) | copy-start | bytes 1540
  122.6 4.9 %copy-start.12 = (pred[32,9]{0,1:T(8,128)(4,1)S(1)}, pred[32,9]{0,1:T(8,128)(4,1)}, u32[]{:S(2)}) copy-start(pred[32,9]{0,1:T(8,128)(4,1)} %constant.194) | copy-start | bytes 868
  165.8 20.8 %collective-permute-start.5 = (bf16[1,1,4,4,64,128]{5,4,2,3,1,0:T(8,128)(2,1)S(1)}, bf16[1,1,4,4,64,128]{5,4,2,3,1,0:T(8,128)(2,1)S(1)}, u32[]{:S(2)}, u32[]{:S(2)}) collective-permute-start(bf16[1,1,4,4,64,128]{5,4,2,3,1,0:T(8,128)(2,1)S(1)} %maximum_bitcast_fusion.3), channel_id=1, source_target_pairs={{16,0},{32,16},{48,32},{64,48},{80,64},{96,80},{112,96},{0,112},{1... | collective-permute-start | bytes 786440 | tf_op jit(solution)/shard_map/ppermute | solution.py:46
  169.8 16.8 %collective-permute-start.4 = (bf16[1,1,4,4,64,128]{5,4,2,3,1,0:T(8,128)(2,1)S(1)}, bf16[1,1,4,4,64,128]{5,4,2,3,1,0:T(8,128)(2,1)S(1)}, u32[]{:S(2)}, u32[]{:S(2)}) collective-permute-start(bf16[1,1,4,4,64,128]{5,4,2,3,1,0:T(8,128)(2,1)S(1)} %maximum_bitcast_fusion.3), channel_id=1, source_target_pairs={{0,16},{16,32},{32,48},{48,64},{64,80},{80,96},{96,112},{112,0},{1... | collective-permute-start | bytes 786440 | tf_op jit(solution)/shard_map/ppermute | solution.py:45
  186.7 19.5 %collective-permute-start.7 = (bf16[3,1,4,4,64,128]{5,4,2,3,1,0:T(8,128)(2,1)S(1)}, bf16[3,1,4,4,64,128]{5,4,2,3,1,0:T(8,128)(2,1)S(1)}, u32[]{:S(2)}, u32[]{:S(2)}) collective-permute-start(bf16[3,1,4,4,64,128]{5,4,2,3,1,0:T(8,128)(2,1)S(1)} %pad_maximum_fusion.3), channel_id=1, source_target_pairs={{1,0},{2,1},{3,2},{4,3},{5,4},{6,5},{7,6},{8,7},{9,8},{10,9},{11,1... | collective-permute-start | bytes 2359304 | tf_op jit(solution)/shard_map/ppermute | solution.py:46
  186.8 19.4 %collective-permute-start.6 = (bf16[3,1,4,4,64,128]{5,4,2,3,1,0:T(8,128)(2,1)S(1)}, bf16[3,1,4,4,64,128]{5,4,2,3,1,0:T(8,128)(2,1)S(1)}, u32[]{:S(2)}, u32[]{:S(2)}) collective-permute-start(bf16[3,1,4,4,64,128]{5,4,2,3,1,0:T(8,128)(2,1)S(1)} %pad_maximum_fusion.3), channel_id=1, source_target_pairs={{0,1},{1,2},{2,3},{3,4},{4,5},{5,6},{6,7},{7,8},{8,9},{9,10},{10,1... | collective-permute-start | bytes 2359304 | tf_op jit(solution)/shard_map/ppermute | solution.py:45
  217.0 4.8 %copy-start.9 = (bf16[3,3,128,128]{3,2,1,0:T(8,128)(2,1)S(1)}, bf16[3,3,128,128]{3,2,1,0:T(8,128)(2,1)}, u32[]{:S(2)}) copy-start(bf16[3,3,128,128]{3,2,1,0:T(8,128)(2,1)} %param.18) | copy-start | bytes 884740
  217.1 4.8 %copy-start.11 = (f32[128]{0:T(128)S(1)}, f32[128]{0:T(128)}, u32[]{:S(2)}) copy-start(f32[128]{0:T(128)} %param.19) | copy-start | bytes 1540
  245.0 4.2 %copy-start.3 = (bf16[4,128,32,128]{3,2,1,0:T(8,128)(2,1)S(1)}, bf16[4,128,32,128]{3,2,1,0:T(8,128)(2,1)}, u32[]{:S(2)}) copy-start(bf16[4,128,32,128]{3,2,1,0:T(8,128)(2,1)} %copy-done.2) | copy-start | bytes 12582916
  245.0 15.0 %copy-start.1 = (bf16[3,3,128,128]{3,2,1,0:T(8,128)(2,1)S(1)}, bf16[3,3,128,128]{3,2,1,0:T(8,128)(2,1)}, u32[]{:S(2)}) copy-start(bf16[3,3,128,128]{3,2,1,0:T(8,128)(2,1)} %param.16) | copy-start | bytes 884740
where the time goes:
time: 265 us; the launch traced here: 260 us
  blocking collectives  63.7 us (24%)
  waiting for transfers between devices  62.6 us (24%)
  matrix products  46.4 us (18%)
  local copies, waits for them, and re-layouts  39.1 us (15%)
  other arithmetic  35.6 us (13%)
  starting transfers between devices  12.1 us (5%)
    all_to_all x1, blocking collectives, shards(): lax.all_to_all(ordered, ('face', 'tile'), split_axis=0, concat_axis=1, ti...  63.7 us
    ppermute x4, waiting for transfers between devices, padded_2(): after = lax.ppermute(first, axis, down)  62.6 us
    conv_general_dilated x2, matrix products, convolve(): lax.conv_general_dilated(padded, weight, (1, 1), 'VALID', dimension_numbe...  46.4 us
    add x2, local copies, waits for them, and re-layouts, convolve(): return summed + bias  13.3 us
    concatenate x2, other arithmetic, pad_tiles(): return jnp.concatenate([upper[:, None], middle, lower[:, None]], 1)  11.7 us
    convert_element_type x1, other arithmetic, shards(): return (nested.astype(jnp.float32) + second).astype(jnp.bfloat16)  10.8 us
    ppermute x4, starting transfers between devices, padded_2(): after = lax.ppermute(first, axis, down)  7.59 us
    unnamed x28, local copies, waits for them, and re-layouts  6.42 us
  transfers between devices with their start and end apart: 8, of which 4 were waited for; matrix products, arithmetic and copies ran while one was open for 0% of the time, Pallas kernels for 0%

commit v1 on v0

v1 whole, which is shorter than its diff:
```python
import jax
import jax.numpy as jnp
import numpy as np
from jax import lax
from jax.experimental import pallas as pl
from jax.experimental.pallas import tpu as pltpu
from jax.sharding import PartitionSpec as P

SIDE = 64
CH = 128
TILES = 4
RANKS = 128
BLOCK = 32
WIDE = 80
LEFT = 8
PAIRS = 8
MESH = pl.DeviceIdType.MESH
BF16, F32 = jnp.bfloat16, jnp.float32

STRIP_TABLE = np.array(
    [
        [1, 2, 0, 3],
        [0, 3, 1, 2],
        [3, 1, 2, 0],
        [2, 0, 3, 1],
        [1, 2, 0, 3],
        [1, 2, 0, 3],
        [0, 3, 1, 2],
        [0, 3, 1, 2],
    ],
    np.int32,
)
FLIP_TABLE = np.array(
    [
        [0, 0, 1, 1],
        [0, 0, 1, 1],
        [0, 1, 1, 0],
        [0, 1, 1, 0],
        [0, 0, 1, 1],
        [0, 0, 1, 1],
        [0, 0, 1, 1],
        [0, 0, 1, 1],
    ],
    np.int32,
)
STEPS = ((-1, 0), (1, 0), (0, -1), (0, 1), (-1, -1), (-1, 1), (1, -1), (1, 1))


def displaced(i):
    f, t = lax.axis_index("face"), lax.axis_index("tile")
    x, c = t // 4, t % 2
    z, y = (f % 2) * 2 + (t // 2) % 2, f // 2
    x = (x + i % 4) % 4
    y = (y + (i // 4) % 4) % 4
    z = (z + (i // 16) % 4) % 4
    c = (c + i // 64) % 2
    return y * 2 + z // 2, x * 4 + (z % 2) * 2 + c


def gelu(v):
    return 0.5 * v * (1.0 + lax.erf(v * np.float32(0.5**0.5)))


def kernel(
    order, table, lat, near, turns, w1, b1, w2, b2, out,
    sent, nested, pad1, pad2, cols, wide1, wide2, lhs, border, edge,
    ask, asked, asked_s, pool, give, get, give_c, get_c,
    send_sem, recv_sem, ask_send, ask_recv, ask_copy, halo_send, halo_recv, corner_send, corner_recv,
):
    face, tile = lax.axis_index("face"), lax.axis_index("tile")
    me = face * 16 + tile

    def beside(k, sign):
        df, dt = STEPS[k]
        return (face + 8 + sign * df) % 8, (tile + 16 + sign * dt) % 16

    def gather(j):
        def step(d8, _):
            for u in range(8):
                d = d8 * 8 + u
                sent[j, d] = lat[order[d * TILES + j]]
            return 0

        lax.fori_loop(0, RANKS // 8, step, 0)
        nested[j, me] = lat[order[me * TILES + j]]

    def send(j):
        def step(i, _):
            f, t = displaced((i * 37) % RANKS)
            pltpu.make_async_remote_copy(
                src_ref=sent.at[j, f * 16 + t],
                dst_ref=nested.at[j, me],
                send_sem=send_sem.at[j],
                recv_sem=recv_sem.at[j],
                device_id=(f, t),
                device_id_type=MESH,
            ).start()
            return 0

        lax.fori_loop(1, RANKS, step, 0)

    def all_of(j):
        view = nested.at[j, pl.ds(0, RANKS - 1)]
        return pltpu.make_async_remote_copy(
            src_ref=view,
            dst_ref=view,
            send_sem=send_sem.at[j],
            recv_sem=recv_sem.at[j],
            device_id=(face, tile),
            device_id_type=MESH,
        )

    ask[...] = jnp.zeros_like(ask)
    ask[0:4, 0:8] = near[...]
    ask[4:8, 0:8] = turns[...]
    gather(0)
    gather(1)
    send(0)
    gather(2)
    send(1)
    gather(3)
    send(2)
    send(3)

    asks = [
        pltpu.make_async_remote_copy(
            src_ref=ask,
            dst_ref=asked.at[k],
            send_sem=ask_send.at[k],
            recv_sem=ask_recv.at[k],
            device_id=beside(k, 1),
            device_id_type=MESH,
        )
        for k in range(8)
    ]
    for a in asks:
        a.start()

    for w, wide in ((w1, wide1), (w2, wide2)):
        zero = jnp.zeros((CH, CH), BF16)
        for q in range(4):
            for dx in range(3):
                at = pl.ds((q * 3 + dx) * CH, CH)
                wide[at, 0:CH] = w[q, dx] if q < 3 else zero
                wide[at, CH : 2 * CH] = w[q - 1, dx] if q > 0 else zero

    for a in asks:
        a.wait()
    fetch = pltpu.make_async_copy(asked, asked_s, ask_copy)
    fetch.start()
    fetch.wait()

    def halo_copies(level):
        copies = []
        for k in range(8):
            copies.append(
                pltpu.make_async_remote_copy(
                    src_ref=give.at[level, k] if k < 4 else give_c.at[level, k - 4],
                    dst_ref=get.at[level, k] if k < 4 else get_c.at[level, k - 4],
                    send_sem=halo_send.at[level, k],
                    recv_sem=halo_recv.at[level, k],
                    device_id=beside(k, -1),
                    device_id_type=MESH,
                )
            )
        return copies

    def pick(level, strips):
        for s in range(16):
            pool[level, s] = strips[s]
        r = lax.broadcasted_iota(jnp.int32, (SIDE, SIDE), 0)
        c = lax.broadcasted_iota(jnp.int32, (SIDE, SIDE), 1)
        mirror = jnp.where(r + c == SIDE - 1, 1.0, 0.0).astype(BF16)
        turned = jnp.dot(mirror, jnp.concatenate(strips, axis=1), preferred_element_type=F32).astype(BF16)
        for s in range(16):
            pool[level, 16 + s] = turned[:, s * CH : (s + 1) * CH]
        for k in range(8):
            for j in range(TILES):
                source = table[k * 4 + asked_s[k, 4 + j, k]] + (asked_s[k, j, k] % TILES) * 4
                if k < 4:
                    give[level, k, j] = pool[level, source]
                elif k % 2 == 0:
                    give_c[level, k - 4, j] = pool[level, source, SIDE - 16 :, :]
                else:
                    give_c[level, k - 4, j] = pool[level, source, 0:16, :]

    def place(level, pad):
        for j in range(TILES):
            flat = pad.at[j].reshape(66 * WIDE, CH)
            pad[j, 0, LEFT : LEFT + SIDE, :] = get[level, 0, j].astype(F32)
            pad[j, 65, LEFT : LEFT + SIDE, :] = get[level, 1, j].astype(F32)
            flat[pl.ds(WIDE + LEFT - 1, SIDE, stride=WIDE), :] = get[level, 2, j].astype(F32)
            flat[pl.ds(WIDE + LEFT + SIDE, SIDE, stride=WIDE), :] = get[level, 3, j].astype(F32)
            for k in range(4):
                block = get_c[level, k, j].astype(F32)
                row = block[15:16] if k % 2 == 0 else block[0:1]
                at_r = 0 if k < 2 else 65
                at_c = LEFT - 1 if k % 2 == 0 else LEFT + SIDE
                pad[j, at_r, at_c : at_c + 1, :] = row

    def columns(j, pad, with_centre):
        def step(r, _):
            if with_centre is not None:
                centre = with_centre(r)
                pad[j, r + 1, LEFT : LEFT + SIDE, :] = centre.astype(F32)
            for dx in range(3):
                cols[dx, (r + 1) // 2, (r + 1) % 2] = pad[j, r + 1, LEFT - 1 + dx : LEFT - 1 + dx + SIDE, :].astype(BF16)
            return 0

        lax.fori_loop(0, SIDE, step, 0)

    def convolve(wide, done):
        def step(b, _):
            p = b * PAIRS
            pieces = []
            for q in range(4):
                for dx in range(3):
                    pieces.append(cols[dx, pl.ds(p + q // 2, PAIRS), q % 2].reshape(PAIRS * SIDE, CH))
            acc = jnp.dot(jnp.concatenate(pieces, axis=1), wide[...], preferred_element_type=F32)
            done(b, acc)
            return 0

        lax.fori_loop(0, SIDE // (2 * PAIRS), step, 0)

    def ring(j, pad, weight, rows):
        flat = pad.at[j].reshape(66 * WIDE, CH)
        n = 4 * rows
        for q in range(3):
            for dx in range(3):
                to = pl.ds((q * 3 + dx) * CH, CH)
                for s in range(n):
                    side, depth = s % 4, s // 4
                    line = depth if side % 2 == 0 else SIDE - 1 - depth
                    if side < 2:
                        v = pad[j, line + q, LEFT - 1 + dx : LEFT - 1 + dx + SIDE, :]
                    else:
                        v = flat[pl.ds(q * WIDE + LEFT - 1 + line + dx, SIDE, stride=WIDE), :]
                    border[s * SIDE : (s + 1) * SIDE, to] = v.astype(BF16)
        return jnp.dot(border[0 : n * SIDE, :], weight, preferred_element_type=F32)

    bias1, bias2 = b1[...], b2[...]
    both1 = jnp.concatenate([bias1, bias1], axis=1)
    both2 = jnp.concatenate([bias2, bias2], axis=1)

    def whole_tile(j, _):
        all_of(j).wait_recv()

        def centre(r):
            return nested[j, pl.ds(2 * r, 2)].reshape(SIDE, CH)

        columns(j, pad1, centre)

        @pl.when(j == TILES - 1)
        def _():
            strips = []
            for i in range(TILES):
                flat = pad1.at[i].reshape(66 * WIDE, CH)
                strips.append(nested[i, 0:2].reshape(SIDE, CH))
                strips.append(nested[i, RANKS - 2 : RANKS].reshape(SIDE, CH))
                strips.append(flat[pl.ds(WIDE + LEFT, SIDE, stride=WIDE), :].astype(BF16))
                strips.append(flat[pl.ds(WIDE + LEFT + SIDE - 1, SIDE, stride=WIDE), :].astype(BF16))
            pick(0, strips)
            for h in halo_copies(0):
                h.start()

        def first_done(b, acc):
            hid = gelu(acc + both1).reshape(PAIRS, SIDE, 2 * CH)
            for p in range(PAIRS):
                row = 2 * (b * PAIRS + p) + 1
                pad2[j, row, LEFT : LEFT + SIDE, :] = hid[p, :, :CH]
                pad2[j, row + 1, LEFT : LEFT + SIDE, :] = hid[p, :, CH:]

        convolve(wide1, first_done)

        @pl.when(j == TILES - 1)
        def _():
            for h in halo_copies(0):
                h.wait_recv()
            place(0, pad1)
            weight = w1[...].reshape(9 * CH, CH)

            def one(i, _):
                hid = gelu(ring(i, pad1, weight, 1) + bias1)
                flat = pad2.at[i].reshape(66 * WIDE, CH)
                pad2[i, 1, LEFT : LEFT + SIDE, :] = hid[0:64]
                pad2[i, SIDE, LEFT : LEFT + SIDE, :] = hid[64:128]
                flat[pl.ds(WIDE + LEFT, SIDE, stride=WIDE), :] = hid[128:192]
                flat[pl.ds(WIDE + LEFT + SIDE - 1, SIDE, stride=WIDE), :] = hid[192:256]
                for s in range(4):
                    edge[i * 4 + s] = hid[s * 64 : (s + 1) * 64].astype(BF16)
                return 0

            lax.fori_loop(0, TILES, one, 0)
            pick(1, [edge[s] for s in range(16)])
            for h in halo_copies(1):
                h.start()

        columns(j, pad2, None)

        def second_done(b, acc):
            acc = (acc + both2).reshape(PAIRS, SIDE, 2 * CH)
            for p in range(PAIRS):
                for half in range(2):
                    row = 2 * (b * PAIRS + p) + half
                    v = acc[p, :, half * CH : (half + 1) * CH] + pad1[j, row + 1, LEFT : LEFT + SIDE, :]
                    out[j, row] = v.astype(BF16)
                    lhs[j, 0, row] = v[0:16]
                    lhs[j, 1, row] = v[SIDE - 16 :]

        convolve(wide2, second_done)
        return 0

    lax.fori_loop(0, TILES, whole_tile, 0)

    for h in halo_copies(1):
        h.wait_recv()
    place(1, pad2)
    weight = w2[...].reshape(9 * CH, CH)

    def last(i, _):
        acc = ring(i, pad2, weight, 2) + bias2
        flat = pad1.at[i].reshape(66 * WIDE, CH)
        for s in range(4, 8):
            pass
        for s in (4, 5, 6, 7, 0, 1, 2, 3):
            side, depth = s % 4, s // 4
            line = depth if side % 2 == 0 else SIDE - 1 - depth
            v = acc[s * SIDE : (s + 1) * SIDE]
            if side < 2:
                v = v + pad1[i, line + 1, LEFT : LEFT + SIDE, :]
                lhs[i, 0, line] = v[0:16]
                lhs[i, 1, line] = v[SIDE - 16 :]
                out[i, line] = v.astype(BF16)
            else:
                v = v + flat[pl.ds(WIDE + LEFT + line, SIDE, stride=WIDE), :]
                block = lhs.at[i, side - 2].reshape(SIDE * 16, CH)
                block[pl.ds(line % 16, SIDE, stride=16), :] = v
        out[i, :, 0:16, :] = lhs[i, 0].astype(BF16)
        out[i, :, SIDE - 16 :, :] = lhs[i, 1].astype(BF16)
        return 0

    lax.fori_loop(0, TILES, last, 0)

    for j in range(TILES):
        all_of(j).wait_send()
    for level in range(2):
        for h in halo_copies(level):
            h.wait_send()


def shards(latitude_rows, tile_order, neighbours, rotations, w_first, b_first, w_second, b_second):
    vmem = pl.BlockSpec(memory_space=pltpu.VMEM)
    smem = pl.BlockSpec(memory_space=pltpu.SMEM)
    table = jnp.asarray((FLIP_TABLE * 16 + STRIP_TABLE).reshape(-1))
    dma = pltpu.SemaphoreType.DMA
    return pl.pallas_call(
        kernel,
        out_shape=jax.ShapeDtypeStruct((TILES, SIDE, SIDE, CH), BF16),
        in_specs=[smem, smem] + [vmem] * 7,
        out_specs=vmem,
        scratch_shapes=[
            pltpu.VMEM((TILES, RANKS, BLOCK, CH), BF16),
            pltpu.VMEM((TILES, RANKS, BLOCK, CH), BF16),
            pltpu.VMEM((TILES, SIDE + 2, WIDE, CH), F32),
            pltpu.VMEM((TILES, SIDE + 2, WIDE, CH), F32),
            pltpu.VMEM((3, SIDE // 2 + 1, 2, SIDE, CH), BF16),
            pltpu.VMEM((12 * CH, 2 * CH), BF16),
            pltpu.VMEM((12 * CH, 2 * CH), BF16),
            pltpu.VMEM((TILES, 2, SIDE, 16, CH), F32),
            pltpu.VMEM((8 * SIDE, 9 * CH), BF16),
            pltpu.VMEM((16, SIDE, CH), BF16),
            pltpu.VMEM((8, CH), jnp.int32),
            pltpu.VMEM((8, 8, CH), jnp.int32),
            pltpu.SMEM((8, 8, CH), jnp.int32),
            pltpu.VMEM((2, 32, SIDE, CH), BF16),
            pltpu.VMEM((2, 4, TILES, SIDE, CH), BF16),
            pltpu.VMEM((2, 4, TILES, SIDE, CH), BF16),
            pltpu.VMEM((2, 4, TILES, 16, CH), BF16),
            pltpu.VMEM((2, 4, TILES, 16, CH), BF16),
            dma((TILES,)),
            dma((TILES,)),
            dma((8,)),
            dma((8,)),
            dma,
            dma((2, 8)),
            dma((2, 8)),
            dma((2, 8)),
            dma((2, 8)),
        ],
        compiler_params=pltpu.CompilerParams(has_side_effects=True, vmem_limit_bytes=62 << 20),
        name="level",
    )(
        tile_order, table, latitude_rows, neighbours, rotations,
        w_first, b_first.reshape(1, CH), w_second, b_second.reshape(1, CH),
    )


def solution(mesh):
    return jax.shard_map(
        shards,
        mesh=mesh,
        in_specs=(
            P(None, ("face", "tile"), None),
            P(),
            P(("face", "tile"), None),
            P(("face", "tile"), None),
            P(),
            P(),
            P(),
            P(),
        ),
        out_specs=P(("face", "tile"), None, None, None),
        check_vma=False,
    )
```

time: 265 us -> 116 us (0.44); the launches traced: 260 us -> 116 us
  Pallas kernels: 0 us -> 111 us
  blocking collectives: 63.7 us -> 0 us
  waiting for transfers between devices: 62.6 us -> 0 us
  matrix products: 46.4 us -> 0 us
  other arithmetic: 35.6 us -> 0 us
  local copies, waits for them, and re-layouts: 39.1 us -> 5.16 us
  starting transfers between devices: 12.1 us -> 0 us
    pallas_call x0 -> x1, Pallas kernels: none -> 111 us  [shards(): pl.pallas_call(kernel, out_shape=jax.ShapeDtypeStruct((TILES, SIDE, SIDE,...]
    all_to_all x1 -> x0, blocking collectives: 63.7 us -> none  [shards(): lax.all_to_all(ordered, ('face', 'tile'), split_axis=0, concat_axis=1, ti...]
    ppermute x8 -> x0, waiting for transfers between devices: 62.6 us -> none  [the longest x4 62.6 us: padded_2(): after = lax.ppermute(first, axis, down)]
    conv_general_dilated x2 -> x0, matrix products: 46.4 us -> none  [convolve(): lax.conv_general_dilated(padded, weight, (1, 1), 'VALID', dimension_numbe...]
    concatenate x6 -> x0, other arithmetic: 13.9 us -> none  [the longest x2 11.7 us: pad_tiles(): return jnp.concatenate([upper[:, None], middle, lower[:, None]], 1)]
    add x2 -> x0, local copies, waits for them, and re-layouts: 13.3 us -> none  [convolve(): return summed + bias]
    ppermute x8 -> x0, starting transfers between devices: 12.1 us -> none  [the longest x4 7.59 us: padded_2(): after = lax.ppermute(first, axis, down)]
    convert_element_type x1 -> x0, other arithmetic: 10.8 us -> none  [shards(): return (nested.astype(jnp.float32) + second).astype(jnp.bfloat16)]
  transfers between devices with their start and end apart: 8 -> 0, of which waited for: 4 -> 0; matrix products, arithmetic and copies ran while one was open for 0% -> 0% of each run, Pallas kernels for 0% -> 0%
where the time goes in v1:
time: 116 us
  Pallas kernels  111 us (96%)
  local copies, waits for them, and re-layouts  5.16 us (4%)
    pallas_call x1, Pallas kernels, shards(): pl.pallas_call(kernel, out_shape=jax.ShapeDtypeStruct((TILES, SIDE, SIDE,...  111 us
    unnamed x1, local copies, waits for them, and re-layouts  5.16 us

profile of v1, /device:TPU:1, one launch (start us, length us, event | category | flops | bytes accessed | tf_op | source)
XLA Modules:
  0.0 116.3 jit_solution(12713682430071075195)
XLA Ops:
  0.0 111.1 %level.1 = bf16[4,64,64,128]{3,2,1,0:T(8,128)(2,1)} custom-call(s32[512]{0:T(512)} %order.1, s32[32]{0:T(128)} %constant.2.clone.table, bf16[512,32,128]{2,1,0:T(8,128)(2,1)} %lat.1, s32[4,8]{1,0:T(4,128)} %near.1, s32[4,8]{1,0:T(4,128)} %turns.1, bf16[3,3,128,128]{3,2,1,0:T(8,128)(2,1)} %w1.1, f32[1,128]{1,0:T(1,128)} %bitcast.2, ...), custom_call_target="tpu_custom_call" | custom-call | tf_op jit(solution)/shard_map/level/pallas_call | solution.py:356
  111.1 5.2 %copy.11 = bf16[4,64,64,128]{3,2,1,0:T(8,128)(2,1)} copy(bf16[4,64,64,128]{3,2,1,0:T(8,128)(2,1)} %level.1) | data formatting | bytes 8388608

commit v2 on v1

--- a/solution.py
+++ b/solution.py
@@ -62,7 +62,8 @@
 
 
 def kernel(
-    order, table, lat, near, turns, w1, b1, w2, b2, out,
+    order_h, table_h, lat_h, near_h, turns_h, w1_h, b1_h, w2_h, b2_h, out,
+    order, table, lat, near, turns, w1, b1, w2, b2, load_sem,
     sent, nested, pad1, pad2, cols, wide1, wide2, lhs, border, edge,
     ask, asked, asked_s, pool, give, get, give_c, get_c,
     send_sem, recv_sem, ask_send, ask_recv, ask_copy, halo_send, halo_recv, corner_send, corner_recv,
@@ -110,18 +111,22 @@
             device_id_type=MESH,
         )
 
+    loads = [
+        pltpu.make_async_copy(src, dst, load_sem.at[i])
+        for i, (src, dst) in enumerate((
+            (order_h, order), (near_h, near), (turns_h, turns), (lat_h, lat), (table_h, table),
+            (w1_h, w1), (b1_h, b1), (w2_h, w2), (b2_h, b2),
+        ))
+    ]
+    for load in loads:
+        load.start()
+    for load in loads[:4]:
+        load.wait()
     ask[...] = jnp.zeros_like(ask)
     ask[0:4, 0:8] = near[...]
     ask[4:8, 0:8] = turns[...]
     gather(0)
     gather(1)
-    send(0)
-    gather(2)
-    send(1)
-    gather(3)
-    send(2)
-    send(3)
-
     asks = [
         pltpu.make_async_remote_copy(
             src_ref=ask,
@@ -136,6 +141,20 @@
     for a in asks:
         a.start()
 
+    send(0)
+    gather(2)
+    send(1)
+    gather(3)
+    send(2)
+    send(3)
+
+    for load in loads[4:]:
+        load.wait()
+
+    for dx in range(3):
+        cols[dx, 0, 0] = jnp.zeros((SIDE, CH), BF16)
+        cols[dx, SIDE // 2, 1] = jnp.zeros((SIDE, CH), BF16)
+
     for w, wide in ((w1, wide1), (w2, wide2)):
         zero = jnp.zeros((CH, CH), BF16)
         for q in range(4):
@@ -143,12 +162,6 @@
                 at = pl.ds((q * 3 + dx) * CH, CH)
                 wide[at, 0:CH] = w[q, dx] if q < 3 else zero
                 wide[at, CH : 2 * CH] = w[q - 1, dx] if q > 0 else zero
-
-    for a in asks:
-        a.wait()
-    fetch = pltpu.make_async_copy(asked, asked_s, ask_copy)
-    fetch.start()
-    fetch.wait()
 
     def halo_copies(level):
         copies = []
@@ -222,21 +235,19 @@
 
         lax.fori_loop(0, SIDE // (2 * PAIRS), step, 0)
 
-    def ring(j, pad, weight, rows):
+    def ring(j, pad, weight, depth):
         flat = pad.at[j].reshape(66 * WIDE, CH)
-        n = 4 * rows
         for q in range(3):
             for dx in range(3):
                 to = pl.ds((q * 3 + dx) * CH, CH)
-                for s in range(n):
-                    side, depth = s % 4, s // 4
-                    line = depth if side % 2 == 0 else SIDE - 1 - depth
-                    if side < 2:
+                for s in range(4):
+                    line = depth if s % 2 == 0 else SIDE - 1 - depth
+                    if s < 2:
                         v = pad[j, line + q, LEFT - 1 + dx : LEFT - 1 + dx + SIDE, :]
                     else:
                         v = flat[pl.ds(q * WIDE + LEFT - 1 + line + dx, SIDE, stride=WIDE), :]
                     border[s * SIDE : (s + 1) * SIDE, to] = v.astype(BF16)
-        return jnp.dot(border[0 : n * SIDE, :], weight, preferred_element_type=F32)
+        return jnp.dot(border[...], weight, preferred_element_type=F32)
 
     bias1, bias2 = b1[...], b2[...]
     both1 = jnp.concatenate([bias1, bias1], axis=1)
@@ -280,7 +291,7 @@
             weight = w1[...].reshape(9 * CH, CH)
 
             def one(i, _):
-                hid = gelu(ring(i, pad1, weight, 1) + bias1)
+                hid = gelu(ring(i, pad1, weight, 0) + bias1)
                 flat = pad2.at[i].reshape(66 * WIDE, CH)
                 pad2[i, 1, LEFT : LEFT + SIDE, :] = hid[0:64]
                 pad2[i, SIDE, LEFT : LEFT + SIDE, :] = hid[64:128]
@@ -310,22 +321,22 @@
         convolve(wide2, second_done)
         return 0
 
+    for a in asks:
+        a.wait()
+    fetch = pltpu.make_async_copy(asked, asked_s, ask_copy)
+    fetch.start()
+    fetch.wait()
+
     lax.fori_loop(0, TILES, whole_tile, 0)
 
-    for h in halo_copies(1):
-        h.wait_recv()
-    place(1, pad2)
     weight = w2[...].reshape(9 * CH, CH)
 
-    def last(i, _):
-        acc = ring(i, pad2, weight, 2) + bias2
+    def mend(i, depth):
+        acc = ring(i, pad2, weight, depth) + bias2
         flat = pad1.at[i].reshape(66 * WIDE, CH)
-        for s in range(4, 8):
-            pass
-        for s in (4, 5, 6, 7, 0, 1, 2, 3):
-            side, depth = s % 4, s // 4
+        for side in (2, 3, 0, 1):
             line = depth if side % 2 == 0 else SIDE - 1 - depth
-            v = acc[s * SIDE : (s + 1) * SIDE]
+            v = acc[side * SIDE : (side + 1) * SIDE]
             if side < 2:
                 v = v + pad1[i, line + 1, LEFT : LEFT + SIDE, :]
                 lhs[i, 0, line] = v[0:16]
@@ -335,11 +346,22 @@
                 v = v + flat[pl.ds(WIDE + LEFT + line, SIDE, stride=WIDE), :]
                 block = lhs.at[i, side - 2].reshape(SIDE * 16, CH)
                 block[pl.ds(line % 16, SIDE, stride=16), :] = v
+
+    def inner_ring(i, _):
+        mend(i, 1)
+        return 0
+
+    def outer_ring(i, _):
+        mend(i, 0)
         out[i, :, 0:16, :] = lhs[i, 0].astype(BF16)
         out[i, :, SIDE - 16 :, :] = lhs[i, 1].astype(BF16)
         return 0
 
-    lax.fori_loop(0, TILES, last, 0)
+    lax.fori_loop(0, TILES, inner_ring, 0)
+    for h in halo_copies(1):
+        h.wait_recv()
+    place(1, pad2)
+    lax.fori_loop(0, TILES, outer_ring, 0)
 
     for j in range(TILES):
         all_of(j).wait_send()
@@ -350,15 +372,24 @@
 
 def shards(latitude_rows, tile_order, neighbours, rotations, w_first, b_first, w_second, b_second):
     vmem = pl.BlockSpec(memory_space=pltpu.VMEM)
-    smem = pl.BlockSpec(memory_space=pltpu.SMEM)
     table = jnp.asarray((FLIP_TABLE * 16 + STRIP_TABLE).reshape(-1))
     dma = pltpu.SemaphoreType.DMA
     return pl.pallas_call(
         kernel,
         out_shape=jax.ShapeDtypeStruct((TILES, SIDE, SIDE, CH), BF16),
-        in_specs=[smem, smem] + [vmem] * 7,
+        in_specs=[pl.BlockSpec(memory_space=pltpu.HBM)] * 9,
         out_specs=vmem,
         scratch_shapes=[
+            pltpu.SMEM((RANKS * TILES,), jnp.int32),
+            pltpu.SMEM((32,), jnp.int32),
+            pltpu.VMEM((RANKS * TILES, BLOCK, CH), BF16),
+            pltpu.VMEM((TILES, 8), jnp.int32),
+            pltpu.VMEM((TILES, 8), jnp.int32),
+            pltpu.VMEM((3, 3, CH, CH), BF16),
+            pltpu.VMEM((1, CH), F32),
+            pltpu.VMEM((3, 3, CH, CH), BF16),
+            pltpu.VMEM((1, CH), F32),
+            dma((9,)),
             pltpu.VMEM((TILES, RANKS, BLOCK, CH), BF16),
             pltpu.VMEM((TILES, RANKS, BLOCK, CH), BF16),
             pltpu.VMEM((TILES, SIDE + 2, WIDE, CH), F32),
@@ -367,7 +398,7 @@
             pltpu.VMEM((12 * CH, 2 * CH), BF16),
             pltpu.VMEM((12 * CH, 2 * CH), BF16),
             pltpu.VMEM((TILES, 2, SIDE, 16, CH), F32),
-            pltpu.VMEM((8 * SIDE, 9 * CH), BF16),
+            pltpu.VMEM((4 * SIDE, 9 * CH), BF16),
             pltpu.VMEM((16, SIDE, CH), BF16),
             pltpu.VMEM((8, CH), jnp.int32),
             pltpu.VMEM((8, 8, CH), jnp.int32),
@@ -387,11 +418,16 @@
             dma((2, 8)),
             dma((2, 8)),
         ],
-        compiler_params=pltpu.CompilerParams(has_side_effects=True, vmem_limit_bytes=62 << 20),
+        compiler_params=pltpu.CompilerParams(has_side_effects=True, vmem_limit_bytes=47 << 20),
         name="level",
     )(
-        tile_order, table, latitude_rows, neighbours, rotations,
-        w_first, b_first.reshape(1, CH), w_second, b_second.reshape(1, CH),
+        *(
+            pltpu.with_memory_space_constraint(v, pltpu.HBM)
+            for v in (
+                tile_order, table, latitude_rows, neighbours, rotations,
+                w_first, b_first.reshape(1, CH), w_second, b_second.reshape(1, CH),
+            )
+        )
     )
 
 

time: 116 us -> 90.4 us (0.78)
  Pallas kernels: 111 us -> 88.3 us
  local copies, waits for them, and re-layouts: 5.16 us -> 2.02 us
    pallas_call x1, Pallas kernels: 111 us -> 88.3 us  [shards(): pl.pallas_call(kernel, out_shape=jax.ShapeDtypeStruct((TILES, SIDE, SIDE,...]
    unnamed x1, local copies, waits for them, and re-layouts: 5.16 us -> 2.02 us
where the time goes in v2:
time: 90.4 us; the launch traced here: 90.3 us
  Pallas kernels  88.3 us (98%)
  local copies, waits for them, and re-layouts  2.02 us (2%)
    pallas_call x1, Pallas kernels, shards(): pl.pallas_call(kernel, out_shape=jax.ShapeDtypeStruct((TILES, SIDE, SIDE,...  88.3 us
    unnamed x1, local copies, waits for them, and re-layouts  2.02 us

profile of v2, /device:TPU:1, one launch (start us, length us, event | category | flops | bytes accessed | tf_op | source)
XLA Modules:
  0.0 90.3 jit_solution(16465947072567853589)
XLA Ops:
  0.0 88.3 %level.1 = bf16[4,64,64,128]{3,2,1,0:T(8,128)(2,1)S(1)} custom-call(s32[512]{0:T(512)} %order_h.1, s32[32]{0:T(128)} %constant.2.clone.table_h, bf16[512,32,128]{2,1,0:T(8,128)(2,1)} %lat_h.1, s32[4,8]{1,0:T(4,128)} %near_h.1, s32[4,8]{1,0:T(4,128)} %turns_h.1, bf16[3,3,128,128]{3,2,1,0:T(8,128)(2,1)} %w1_h.1, f32[1,128]{1,0:T(1,128)} %bitcast.2, ...), custom_call_target="tpu_custom_call" | custom-call | tf_op jit(solution)/shard_map/level/pallas_call | solution.py:377
  88.3 2.0 %copy.11 = bf16[4,64,64,128]{3,2,1,0:T(8,128)(2,1)} copy(bf16[4,64,64,128]{3,2,1,0:T(8,128)(2,1)S(1)} %level.1) | data formatting | bytes 8388608

commit v3 on v2

--- a/solution.py
+++ b/solution.py
@@ -63,13 +63,17 @@
 
 def kernel(
     order_h, table_h, lat_h, near_h, turns_h, w1_h, b1_h, w2_h, b2_h, out,
-    order, table, lat, near, turns, w1, b1, w2, b2, load_sem,
-    sent, nested, pad1, pad2, cols, wide1, wide2, lhs, border, edge,
+    order, table, area, near, turns, w1, b1, w2, b2, load_sem,
+    sent, nested, pad1, pad2, wide1, wide2, lhs, border,
+    lines, beyond, part_row, part_col, flat_tmp,
     ask, asked, asked_s, pool, give, get, give_c, get_c,
     send_sem, recv_sem, ask_send, ask_recv, ask_copy, halo_send, halo_recv, corner_send, corner_recv,
 ):
     face, tile = lax.axis_index("face"), lax.axis_index("tile")
     me = face * 16 + tile
+    lat = area.reshape(RANKS * TILES, BLOCK, CH)
+    cols = area.reshape(RANKS, 2, SIDE, CH)
+    pairs = SIDE // 2 + 1
 
     def beside(k, sign):
         df, dt = STEPS[k]
@@ -151,9 +155,20 @@
     for load in loads[4:]:
         load.wait()
 
+    for pad in (pad1, pad2):
+        for j in range(TILES):
+            flat = pad.at[j].reshape(66 * WIDE, CH)
+            for at_c in (LEFT - 1, LEFT + SIDE):
+                flat[pl.ds(WIDE + at_c, SIDE, stride=WIDE), :] = jnp.zeros((SIDE, CH), F32)
+    for j in range(TILES):
+        pad2[j, 0] = jnp.zeros((WIDE, CH), F32)
+        pad2[j, 65] = jnp.zeros((WIDE, CH), F32)
+        for side in (2, 3):
+            lines[j, side, 0:8] = jnp.zeros((8, CH), F32)
+            lines[j, side, LEFT + SIDE :] = jnp.zeros((8, CH), F32)
     for dx in range(3):
-        cols[dx, 0, 0] = jnp.zeros((SIDE, CH), BF16)
-        cols[dx, SIDE // 2, 1] = jnp.zeros((SIDE, CH), BF16)
+        cols[dx * pairs, 0] = jnp.zeros((SIDE, CH), BF16)
+        cols[dx * pairs + SIDE // 2, 1] = jnp.zeros((SIDE, CH), BF16)
 
     for w, wide in ((w1, wide1), (w2, wide2)):
         zero = jnp.zeros((CH, CH), BF16)
@@ -178,38 +193,84 @@
             )
         return copies
 
-    def pick(level, strips):
-        for s in range(16):
-            pool[level, s] = strips[s]
+    def turn(level, first, strips):
         r = lax.broadcasted_iota(jnp.int32, (SIDE, SIDE), 0)
         c = lax.broadcasted_iota(jnp.int32, (SIDE, SIDE), 1)
         mirror = jnp.where(r + c == SIDE - 1, 1.0, 0.0).astype(BF16)
         turned = jnp.dot(mirror, jnp.concatenate(strips, axis=1), preferred_element_type=F32).astype(BF16)
-        for s in range(16):
-            pool[level, 16 + s] = turned[:, s * CH : (s + 1) * CH]
+        for s in range(len(strips)):
+            pool[level, first + s] = strips[s]
+            pool[level, 16 + first + s] = turned[:, s * CH : (s + 1) * CH]
+
+    def pick(level):
+        at = lax.broadcasted_iota(jnp.int32, (16, CH), 0)
         for k in range(8):
+            ends = jnp.zeros((16, CH), F32)
             for j in range(TILES):
                 source = table[k * 4 + asked_s[k, 4 + j, k]] + (asked_s[k, j, k] % TILES) * 4
                 if k < 4:
                     give[level, k, j] = pool[level, source]
                 elif k % 2 == 0:
-                    give_c[level, k - 4, j] = pool[level, source, SIDE - 16 :, :]
+                    ends = jnp.where(at == j, pool[level, source, SIDE - 16 :, :].astype(F32)[15:16], ends)
                 else:
-                    give_c[level, k - 4, j] = pool[level, source, 0:16, :]
-
-    def place(level, pad):
+                    ends = jnp.where(at == j, pool[level, source, 0:16, :].astype(F32)[0:1], ends)
+            if k >= 4:
+                give_c[level, k - 4] = ends.astype(BF16)
+
+    def halo_terms(level, w):
+        for k in range(4):
+            ends = get_c[level, k].astype(F32)
+            for j in range(TILES):
+                lines[j, k, LEFT : LEFT + SIDE] = get[level, k, j].astype(F32)
+                at_c = LEFT - 1 if k % 2 == 0 else LEFT + SIDE
+                lines[j, k // 2, at_c : at_c + 1] = ends[j : j + 1]
+        sums = []
+        for side, taps in enumerate((w[0], w[2], w[:, 0], w[:, 2])):
+            for j in range(TILES):
+                for n in range(3):
+                    beyond[side, j * SIDE : (j + 1) * SIDE, n * CH : (n + 1) * CH] = lines[
+                        j, side, LEFT - 1 + n : LEFT - 1 + n + SIDE
+                    ].astype(BF16)
+            sums.append(jnp.dot(beyond[side], taps.reshape(3 * CH, CH), preferred_element_type=F32))
+        r = lax.broadcasted_iota(jnp.int32, (SIDE, CH), 0)
+
+        def both_ends(v, first, last):
+            return v + jnp.where(r == 0, first, 0.0) + jnp.where(r == SIDE - 1, last, 0.0)
+
+        terms = []
         for j in range(TILES):
-            flat = pad.at[j].reshape(66 * WIDE, CH)
-            pad[j, 0, LEFT : LEFT + SIDE, :] = get[level, 0, j].astype(F32)
-            pad[j, 65, LEFT : LEFT + SIDE, :] = get[level, 1, j].astype(F32)
-            flat[pl.ds(WIDE + LEFT - 1, SIDE, stride=WIDE), :] = get[level, 2, j].astype(F32)
-            flat[pl.ds(WIDE + LEFT + SIDE, SIDE, stride=WIDE), :] = get[level, 3, j].astype(F32)
-            for k in range(4):
-                block = get_c[level, k, j].astype(F32)
-                row = block[15:16] if k % 2 == 0 else block[0:1]
-                at_r = 0 if k < 2 else 65
-                at_c = LEFT - 1 if k % 2 == 0 else LEFT + SIDE
-                pad[j, at_r, at_c : at_c + 1, :] = row
+            up, low, left, right = (v[j * SIDE : (j + 1) * SIDE] for v in sums)
+            terms.append((
+                both_ends(up, left[0:1], right[0:1]),
+                both_ends(low, left[SIDE - 1 :], right[SIDE - 1 :]),
+                both_ends(left, up[0:1], low[0:1]),
+                both_ends(right, up[SIDE - 1 :], low[SIDE - 1 :]),
+            ))
+        return terms
+
+    def keep_edges(j, b, acc):
+        @pl.when(b == 0)
+        def _():
+            part_row[j, 0] = acc[0, :, :CH]
+
+        @pl.when(b == SIDE // (2 * PAIRS) - 1)
+        def _():
+            part_row[j, 1] = acc[PAIRS - 1, :, CH:]
+
+        for p in range(PAIRS):
+            for half in range(2):
+                lanes = slice(half * CH, (half + 1) * CH)
+                n = 2 * p + half
+                part_col[j, 0, b, n : n + 1] = acc[p, 0:1, lanes]
+                part_col[j, 1, b, n : n + 1] = acc[p, SIDE - 1 :, lanes]
+
+    def edges(j):
+        return (
+            part_row[j, 0],
+            part_row[j, 1],
+            part_col[j, 0].reshape(SIDE, CH),
+            part_col[j, 1].reshape(SIDE, CH),
+        )
 
     def columns(j, pad, with_centre):
         def step(r, _):
@@ -217,7 +278,7 @@
                 centre = with_centre(r)
                 pad[j, r + 1, LEFT : LEFT + SIDE, :] = centre.astype(F32)
             for dx in range(3):
-                cols[dx, (r + 1) // 2, (r + 1) % 2] = pad[j, r + 1, LEFT - 1 + dx : LEFT - 1 + dx + SIDE, :].astype(BF16)
+                area[dx * 2 * pairs + r + 1] = pad[j, r + 1, LEFT - 1 + dx : LEFT - 1 + dx + SIDE, :].astype(BF16)
             return 0
 
         lax.fori_loop(0, SIDE, step, 0)
@@ -228,7 +289,7 @@
             pieces = []
             for q in range(4):
                 for dx in range(3):
-                    pieces.append(cols[dx, pl.ds(p + q // 2, PAIRS), q % 2].reshape(PAIRS * SIDE, CH))
+                    pieces.append(cols[pl.ds(p + dx * pairs + q // 2, PAIRS), q % 2].reshape(PAIRS * SIDE, CH))
             acc = jnp.dot(jnp.concatenate(pieces, axis=1), wide[...], preferred_element_type=F32)
             done(b, acc)
             return 0
@@ -259,23 +320,26 @@
         def centre(r):
             return nested[j, pl.ds(2 * r, 2)].reshape(SIDE, CH)
 
-        columns(j, pad1, centre)
+        halves = nested.at[j].reshape(SIDE, 2, BLOCK, CH)
+        strips = [nested[j, 0:2].reshape(SIDE, CH), nested[j, RANKS - 2 : RANKS].reshape(SIDE, CH)]
+        for side in range(2):
+            block = (halves[:, 1, 16:32, :] if side else halves[:, 0, 0:16, :]).astype(F32)
+            flat_tmp[side] = (block[:, 8:16] if side else block[:, 0:8]).reshape(SIDE * 8, CH)
+            strips.append(flat_tmp[side, pl.ds(7 * side, SIDE, stride=8), :].astype(BF16))
+        turn(0, j * 4, strips)
 
         @pl.when(j == TILES - 1)
         def _():
-            strips = []
-            for i in range(TILES):
-                flat = pad1.at[i].reshape(66 * WIDE, CH)
-                strips.append(nested[i, 0:2].reshape(SIDE, CH))
-                strips.append(nested[i, RANKS - 2 : RANKS].reshape(SIDE, CH))
-                strips.append(flat[pl.ds(WIDE + LEFT, SIDE, stride=WIDE), :].astype(BF16))
-                strips.append(flat[pl.ds(WIDE + LEFT + SIDE - 1, SIDE, stride=WIDE), :].astype(BF16))
-            pick(0, strips)
+            pick(0)
             for h in halo_copies(0):
                 h.start()
 
+        columns(j, pad1, centre)
+
         def first_done(b, acc):
-            hid = gelu(acc + both1).reshape(PAIRS, SIDE, 2 * CH)
+            acc = (acc + both1).reshape(PAIRS, SIDE, 2 * CH)
+            keep_edges(j, b, acc)
+            hid = gelu(acc)
             for p in range(PAIRS):
                 row = 2 * (b * PAIRS + p) + 1
                 pad2[j, row, LEFT : LEFT + SIDE, :] = hid[p, :, :CH]
@@ -287,22 +351,16 @@
         def _():
             for h in halo_copies(0):
                 h.wait_recv()
-            place(0, pad1)
-            weight = w1[...].reshape(9 * CH, CH)
-
-            def one(i, _):
-                hid = gelu(ring(i, pad1, weight, 0) + bias1)
+            terms = halo_terms(0, w1)
+            for i in range(TILES):
                 flat = pad2.at[i].reshape(66 * WIDE, CH)
-                pad2[i, 1, LEFT : LEFT + SIDE, :] = hid[0:64]
-                pad2[i, SIDE, LEFT : LEFT + SIDE, :] = hid[64:128]
-                flat[pl.ds(WIDE + LEFT, SIDE, stride=WIDE), :] = hid[128:192]
-                flat[pl.ds(WIDE + LEFT + SIDE - 1, SIDE, stride=WIDE), :] = hid[192:256]
-                for s in range(4):
-                    edge[i * 4 + s] = hid[s * 64 : (s + 1) * 64].astype(BF16)
-                return 0
-
-            lax.fori_loop(0, TILES, one, 0)
-            pick(1, [edge[s] for s in range(16)])
+                hid = [gelu(part + term) for part, term in zip(edges(i), terms[i])]
+                pad2[i, 1, LEFT : LEFT + SIDE, :] = hid[0]
+                pad2[i, SIDE, LEFT : LEFT + SIDE, :] = hid[1]
+                flat[pl.ds(WIDE + LEFT, SIDE, stride=WIDE), :] = hid[2]
+                flat[pl.ds(WIDE + LEFT + SIDE - 1, SIDE, stride=WIDE), :] = hid[3]
+                turn(1, i * 4, [h.astype(BF16) for h in hid])
+            pick(1)
             for h in halo_copies(1):
                 h.start()
 
@@ -310,6 +368,11 @@
 
         def second_done(b, acc):
             acc = (acc + both2).reshape(PAIRS, SIDE, 2 * CH)
+
+            @pl.when(j == TILES - 1)
+            def _():
+                keep_edges(j, b, acc)
+
             for p in range(PAIRS):
                 for half in range(2):
                     row = 2 * (b * PAIRS + p) + half
@@ -331,12 +394,11 @@
 
     weight = w2[...].reshape(9 * CH, CH)
 
-    def mend(i, depth):
-        acc = ring(i, pad2, weight, depth) + bias2
+    def finish(i, depth, values):
         flat = pad1.at[i].reshape(66 * WIDE, CH)
         for side in (2, 3, 0, 1):
             line = depth if side % 2 == 0 else SIDE - 1 - depth
-            v = acc[side * SIDE : (side + 1) * SIDE]
+            v = values[side]
             if side < 2:
                 v = v + pad1[i, line + 1, LEFT : LEFT + SIDE, :]
                 lhs[i, 0, line] = v[0:16]
@@ -347,21 +409,24 @@
                 block = lhs.at[i, side - 2].reshape(SIDE * 16, CH)
                 block[pl.ds(line % 16, SIDE, stride=16), :] = v
 
-    def inner_ring(i, _):
-        mend(i, 1)
+    def rings(i, _):
+        acc = ring(i, pad2, weight, 1) + bias2
+        finish(i, 1, [acc[s * SIDE : (s + 1) * SIDE] for s in range(4)])
+        acc = ring(i, pad2, weight, 0) + bias2
+        part_row[i, 0] = acc[0:SIDE]
+        part_row[i, 1] = acc[SIDE : 2 * SIDE]
+        for side in range(2):
+            part_col[i, side] = acc[(2 + side) * SIDE : (3 + side) * SIDE].reshape(SIDE // 16, 16, CH)
         return 0
 
-    def outer_ring(i, _):
-        mend(i, 0)
+    lax.fori_loop(0, TILES - 1, rings, 0)
+    for h in halo_copies(1):
+        h.wait_recv()
+    terms = halo_terms(1, w2)
+    for i in range(TILES):
+        finish(i, 0, [part + term for part, term in zip(edges(i), terms[i])])
         out[i, :, 0:16, :] = lhs[i, 0].astype(BF16)
         out[i, :, SIDE - 16 :, :] = lhs[i, 1].astype(BF16)
-        return 0
-
-    lax.fori_loop(0, TILES, inner_ring, 0)
-    for h in halo_copies(1):
-        h.wait_recv()
-    place(1, pad2)
-    lax.fori_loop(0, TILES, outer_ring, 0)
 
     for j in range(TILES):
         all_of(j).wait_send()
@@ -382,7 +447,7 @@
         scratch_shapes=[
             pltpu.SMEM((RANKS * TILES,), jnp.int32),
             pltpu.SMEM((32,), jnp.int32),
-            pltpu.VMEM((RANKS * TILES, BLOCK, CH), BF16),
+            pltpu.VMEM((RANKS * TILES * BLOCK // SIDE, SIDE, CH), BF16),
             pltpu.VMEM((TILES, 8), jnp.int32),
             pltpu.VMEM((TILES, 8), jnp.int32),
             pltpu.VMEM((3, 3, CH, CH), BF16),
@@ -394,20 +459,23 @@
             pltpu.VMEM((TILES, RANKS, BLOCK, CH), BF16),
             pltpu.VMEM((TILES, SIDE + 2, WIDE, CH), F32),
             pltpu.VMEM((TILES, SIDE + 2, WIDE, CH), F32),
-            pltpu.VMEM((3, SIDE // 2 + 1, 2, SIDE, CH), BF16),
             pltpu.VMEM((12 * CH, 2 * CH), BF16),
             pltpu.VMEM((12 * CH, 2 * CH), BF16),
             pltpu.VMEM((TILES, 2, SIDE, 16, CH), F32),
             pltpu.VMEM((4 * SIDE, 9 * CH), BF16),
-            pltpu.VMEM((16, SIDE, CH), BF16),
+            pltpu.VMEM((TILES, 4, WIDE, CH), F32),
+            pltpu.VMEM((4, TILES * SIDE, 3 * CH), BF16),
+            pltpu.VMEM((TILES, 2, SIDE, CH), F32),
+            pltpu.VMEM((TILES, 2, SIDE // 16, 16, CH), F32),
+            pltpu.VMEM((2, SIDE * 8, CH), F32),
             pltpu.VMEM((8, CH), jnp.int32),
             pltpu.VMEM((8, 8, CH), jnp.int32),
             pltpu.SMEM((8, 8, CH), jnp.int32),
             pltpu.VMEM((2, 32, SIDE, CH), BF16),
             pltpu.VMEM((2, 4, TILES, SIDE, CH), BF16),
             pltpu.VMEM((2, 4, TILES, SIDE, CH), BF16),
-            pltpu.VMEM((2, 4, TILES, 16, CH), BF16),
-            pltpu.VMEM((2, 4, TILES, 16, CH), BF16),
+            pltpu.VMEM((2, 4, 16, CH), BF16),
+            pltpu.VMEM((2, 4, 16, CH), BF16),
             dma((TILES,)),
             dma((TILES,)),
             dma((8,)),
@@ -418,7 +486,7 @@
             dma((2, 8)),
             dma((2, 8)),
         ],
-        compiler_params=pltpu.CompilerParams(has_side_effects=True, vmem_limit_bytes=47 << 20),
+        compiler_params=pltpu.CompilerParams(has_side_effects=True, vmem_limit_bytes=48 << 20),
         name="level",
     )(
         *(

time: 90.4 us -> 85.4 us (0.945)
  Pallas kernels: 88.3 us -> 83.2 us
    pallas_call x1, Pallas kernels: 88.3 us -> 83.2 us  [shards(): pl.pallas_call(kernel, out_shape=jax.ShapeDtypeStruct((TILES, SIDE, SIDE,...]
where the time goes in v3:
time: 85.4 us; the launch traced here: 85.3 us
  Pallas kernels  83.2 us (97%)
  local copies, waits for them, and re-layouts  2.02 us (2%)
    pallas_call x1, Pallas kernels, shards(): pl.pallas_call(kernel, out_shape=jax.ShapeDtypeStruct((TILES, SIDE, SIDE,...  83.2 us
    unnamed x1, local copies, waits for them, and re-layouts  2.02 us

profile of v3, /device:TPU:1, one launch (start us, length us, event | category | flops | bytes accessed | tf_op | source)
XLA Modules:
  0.0 85.3 jit_solution(17523722945984700946)
XLA Ops:
  0.0 83.2 %level.1 = bf16[4,64,64,128]{3,2,1,0:T(8,128)(2,1)S(1)} custom-call(s32[512]{0:T(512)} %order_h.1, s32[32]{0:T(128)} %constant.2.clone.table_h, bf16[512,32,128]{2,1,0:T(8,128)(2,1)} %lat_h.1, s32[4,8]{1,0:T(4,128)} %near_h.1, s32[4,8]{1,0:T(4,128)} %turns_h.1, bf16[3,3,128,128]{3,2,1,0:T(8,128)(2,1)} %w1_h.1, f32[1,128]{1,0:T(1,128)} %bitcast.2, ...), custom_call_target="tpu_custom_call" | custom-call | tf_op jit(solution)/shard_map/level/pallas_call | solution.py:442
  83.2 2.0 %copy.11 = bf16[4,64,64,128]{3,2,1,0:T(8,128)(2,1)} copy(bf16[4,64,64,128]{3,2,1,0:T(8,128)(2,1)S(1)} %level.1) | data formatting | bytes 8388608

commit v4 on v3

--- a/solution.py
+++ b/solution.py
@@ -46,6 +46,18 @@
 STEPS = ((-1, 0), (1, 0), (0, -1), (0, 1), (-1, -1), (-1, 1), (1, -1), (1, 1))
 
 
+def places():
+    f, t = lax.axis_index("face"), lax.axis_index("tile")
+    x, c = t // 4, t % 2
+    z, y = (f % 2) * 2 + (t // 2) % 2, f // 2
+    xs, ys, zs = ([(v + d) % 4 for d in range(4)] for v in (x, y, z))
+    cs = [c, (c + 1) % 2]
+    faces = [[b * 2 + a // 2 for a in zs] for b in ys]
+    tiles = [[[b * 4 + (a % 2) * 2 + e for e in cs] for a in zs] for b in xs]
+    far = (2, 1, 3, 0)
+    return [(faces[dy][dz], tiles[dx][dz][dc]) for dx in far for dy in far for dz in far for dc in (1, 0)]
+
+
 def displaced(i):
     f, t = lax.axis_index("face"), lax.axis_index("tile")
     x, c = t // 4, t % 2
@@ -65,7 +77,7 @@
     order_h, table_h, lat_h, near_h, turns_h, w1_h, b1_h, w2_h, b2_h, out,
     order, table, area, near, turns, w1, b1, w2, b2, load_sem,
     sent, nested, pad1, pad2, wide1, wide2, lhs, border,
-    lines, beyond, part_row, part_col, flat_tmp,
+    which, near_edge, lines, beyond, part_row, part_col, flat_tmp,
     ask, asked, asked_s, pool, give, get, give_c, get_c,
     send_sem, recv_sem, ask_send, ask_recv, ask_copy, halo_send, halo_recv, corner_send, corner_recv,
 ):
@@ -124,6 +136,9 @@
     ]
     for load in loads:
         load.start()
+    ready = pltpu.get_barrier_semaphore()
+    for step in places()[:-1]:
+        pl.semaphore_signal(ready, inc=1, device_id=step, device_id_type=MESH)
     for load in loads[:4]:
         load.wait()
     ask[...] = jnp.zeros_like(ask)
@@ -131,6 +146,7 @@
     ask[4:8, 0:8] = turns[...]
     gather(0)
     gather(1)
+    pl.semaphore_wait(ready, RANKS - 1)
     asks = [
         pltpu.make_async_remote_copy(
             src_ref=ask,
@@ -160,6 +176,10 @@
             flat = pad.at[j].reshape(66 * WIDE, CH)
             for at_c in (LEFT - 1, LEFT + SIDE):
                 flat[pl.ds(WIDE + at_c, SIDE, stride=WIDE), :] = jnp.zeros((SIDE, CH), F32)
+    for side in range(2):
+        for n in range(3):
+            near_edge[side, n, 0:8] = jnp.zeros((8, CH), F32)
+            near_edge[side, n, LEFT + SIDE :] = jnp.zeros((8, CH), F32)
     for j in range(TILES):
         pad2[j, 0] = jnp.zeros((WIDE, CH), F32)
         pad2[j, 65] = jnp.zeros((WIDE, CH), F32)
@@ -180,7 +200,7 @@
 
     def halo_copies(level):
         copies = []
-        for k in range(8):
+        for k in (4, 5, 6, 7, 0, 1, 2, 3):
             copies.append(
                 pltpu.make_async_remote_copy(
                     src_ref=give.at[level, k] if k < 4 else give_c.at[level, k - 4],
@@ -204,10 +224,10 @@
 
     def pick(level):
         at = lax.broadcasted_iota(jnp.int32, (16, CH), 0)
-        for k in range(8):
+        for k in (4, 5, 6, 7, 0, 1, 2, 3):
             ends = jnp.zeros((16, CH), F32)
             for j in range(TILES):
-                source = table[k * 4 + asked_s[k, 4 + j, k]] + (asked_s[k, j, k] % TILES) * 4
+                source = which[k * TILES + j]
                 if k < 4:
                     give[level, k, j] = pool[level, source]
                 elif k % 2 == 0:
@@ -296,18 +316,26 @@
 
         lax.fori_loop(0, SIDE // (2 * PAIRS), step, 0)
 
-    def ring(j, pad, weight, depth):
+    def ring(j, pad, weight):
         flat = pad.at[j].reshape(66 * WIDE, CH)
-        for q in range(3):
-            for dx in range(3):
-                to = pl.ds((q * 3 + dx) * CH, CH)
-                for s in range(4):
-                    line = depth if s % 2 == 0 else SIDE - 1 - depth
-                    if s < 2:
-                        v = pad[j, line + q, LEFT - 1 + dx : LEFT - 1 + dx + SIDE, :]
-                    else:
-                        v = flat[pl.ds(q * WIDE + LEFT - 1 + line + dx, SIDE, stride=WIDE), :]
-                    border[s * SIDE : (s + 1) * SIDE, to] = v.astype(BF16)
+        for side in range(2):
+            for n in range(3):
+                c = SIDE - 1 - n if side else n
+                near_edge[side, n, LEFT : LEFT + SIDE] = flat[pl.ds(WIDE + LEFT + c, SIDE, stride=WIDE), :]
+        for depth in range(2):
+            for s in range(4):
+                at = slice((depth * 4 + s) * SIDE, (depth * 4 + s + 1) * SIDE)
+                line = depth if s % 2 == 0 else SIDE - 1 - depth
+                for q in range(3):
+                    for dx in range(3):
+                        n = depth + (dx - 1 if s == 2 else 1 - dx)
+                        if s < 2:
+                            v = pad[j, line + q, LEFT - 1 + dx : LEFT - 1 + dx + SIDE, :].astype(BF16)
+                        elif n < 0:
+                            v = jnp.zeros((SIDE, CH), BF16)
+                        else:
+                            v = near_edge[s - 2, n, LEFT - 1 + q : LEFT - 1 + q + SIDE].astype(BF16)
+                        border[at, (q * 3 + dx) * CH : (q * 3 + dx + 1) * CH] = v
         return jnp.dot(border[...], weight, preferred_element_type=F32)
 
     bias1, bias2 = b1[...], b2[...]
@@ -353,16 +381,16 @@
                 h.wait_recv()
             terms = halo_terms(0, w1)
             for i in range(TILES):
-                flat = pad2.at[i].reshape(66 * WIDE, CH)
-                hid = [gelu(part + term) for part, term in zip(edges(i), terms[i])]
-                pad2[i, 1, LEFT : LEFT + SIDE, :] = hid[0]
-                pad2[i, SIDE, LEFT : LEFT + SIDE, :] = hid[1]
-                flat[pl.ds(WIDE + LEFT, SIDE, stride=WIDE), :] = hid[2]
-                flat[pl.ds(WIDE + LEFT + SIDE - 1, SIDE, stride=WIDE), :] = hid[3]
-                turn(1, i * 4, [h.astype(BF16) for h in hid])
+                turn(1, i * 4, [gelu(part + term).astype(BF16) for part, term in zip(edges(i), terms[i])])
             pick(1)
             for h in halo_copies(1):
                 h.start()
+            for i in range(TILES):
+                flat = pad2.at[i].reshape(66 * WIDE, CH)
+                pad2[i, 1, LEFT : LEFT + SIDE, :] = pool[1, i * 4].astype(F32)
+                pad2[i, SIDE, LEFT : LEFT + SIDE, :] = pool[1, i * 4 + 1].astype(F32)
+                flat[pl.ds(WIDE + LEFT, SIDE, stride=WIDE), :] = pool[1, i * 4 + 2].astype(F32)
+                flat[pl.ds(WIDE + LEFT + SIDE - 1, SIDE, stride=WIDE), :] = pool[1, i * 4 + 3].astype(F32)
 
         columns(j, pad2, None)
 
@@ -389,6 +417,9 @@
     fetch = pltpu.make_async_copy(asked, asked_s, ask_copy)
     fetch.start()
     fetch.wait()
+    for k in range(8):
+        for j in range(TILES):
+            which[k * TILES + j] = table[k * 4 + asked_s[k, 4 + j, k]] + (asked_s[k, j, k] % TILES) * 4
 
     lax.fori_loop(0, TILES, whole_tile, 0)
 
@@ -410,9 +441,8 @@
                 block[pl.ds(line % 16, SIDE, stride=16), :] = v
 
     def rings(i, _):
-        acc = ring(i, pad2, weight, 1) + bias2
-        finish(i, 1, [acc[s * SIDE : (s + 1) * SIDE] for s in range(4)])
-        acc = ring(i, pad2, weight, 0) + bias2
+        acc = ring(i, pad2, weight) + bias2
+        finish(i, 1, [acc[(4 + s) * SIDE : (5 + s) * SIDE] for s in range(4)])
         part_row[i, 0] = acc[0:SIDE]
         part_row[i, 1] = acc[SIDE : 2 * SIDE]
         for side in range(2):
@@ -462,7 +492,9 @@
             pltpu.VMEM((12 * CH, 2 * CH), BF16),
             pltpu.VMEM((12 * CH, 2 * CH), BF16),
             pltpu.VMEM((TILES, 2, SIDE, 16, CH), F32),
-            pltpu.VMEM((4 * SIDE, 9 * CH), BF16),
+            pltpu.VMEM((8 * SIDE, 9 * CH), BF16),
+            pltpu.SMEM((8 * TILES,), jnp.int32),
+            pltpu.VMEM((2, 3, WIDE, CH), F32),
             pltpu.VMEM((TILES, 4, WIDE, CH), F32),
             pltpu.VMEM((4, TILES * SIDE, 3 * CH), BF16),
             pltpu.VMEM((TILES, 2, SIDE, CH), F32),
@@ -486,7 +518,7 @@
             dma((2, 8)),
             dma((2, 8)),
         ],
-        compiler_params=pltpu.CompilerParams(has_side_effects=True, vmem_limit_bytes=48 << 20),
+        compiler_params=pltpu.CompilerParams(collective_id=0, has_side_effects=True, vmem_limit_bytes=48 << 20),
         name="level",
     )(
         *(

time: 85.4 us -> 76.6 us (0.90)
  Pallas kernels: 83.2 us -> 74.5 us
    pallas_call x1, Pallas kernels: 83.2 us -> 74.5 us  [shards(): pl.pallas_call(kernel, out_shape=jax.ShapeDtypeStruct((TILES, SIDE, SIDE,...]
where the time goes in v4:
time: 76.6 us; the launch traced here: 76.5 us
  Pallas kernels  74.5 us (97%)
  local copies, waits for them, and re-layouts  2.02 us (3%)
    pallas_call x1, Pallas kernels, shards(): pl.pallas_call(kernel, out_shape=jax.ShapeDtypeStruct((TILES, SIDE, SIDE,...  74.5 us
    unnamed x1, local copies, waits for them, and re-layouts  2.02 us

profile of v4, /device:TPU:1, one launch (start us, length us, event | category | flops | bytes accessed | tf_op | source)
XLA Modules:
  0.0 76.5 jit_solution(8888899190575671247)
XLA Ops:
  0.0 74.5 %level.1 = bf16[4,64,64,128]{3,2,1,0:T(8,128)(2,1)S(1)} custom-call(s32[512]{0:T(512)} %order_h.1, s32[32]{0:T(128)} %constant.2.clone.table_h, bf16[512,32,128]{2,1,0:T(8,128)(2,1)} %lat_h.1, s32[4,8]{1,0:T(4,128)} %near_h.1, s32[4,8]{1,0:T(4,128)} %turns_h.1, bf16[3,3,128,128]{3,2,1,0:T(8,128)(2,1)} %w1_h.1, f32[1,128]{1,0:T(1,128)} %bitcast.2, ...), custom_call_target="tpu_custom_call" | custom-call | tf_op jit(solution)/shard_map/level/pallas_call | solution.py:472
  74.5 2.0 %copy.11 = bf16[4,64,64,128]{3,2,1,0:T(8,128)(2,1)} copy(bf16[4,64,64,128]{3,2,1,0:T(8,128)(2,1)S(1)} %level.1) | data formatting | bytes 8388608

commit v5 on v4

--- a/solution.py
+++ b/solution.py
@@ -127,10 +127,12 @@
             device_id_type=MESH,
         )
 
+    quarters = [pl.ds(q * RANKS, RANKS) for q in range(4)]
     loads = [
         pltpu.make_async_copy(src, dst, load_sem.at[i])
         for i, (src, dst) in enumerate((
-            (order_h, order), (near_h, near), (turns_h, turns), (lat_h, lat), (table_h, table),
+            (order_h, order), (near_h, near), (turns_h, turns),
+            *((lat_h.at[q], lat.at[q]) for q in quarters), (table_h, table),
             (w1_h, w1), (b1_h, b1), (w2_h, w2), (b2_h, b2),
         ))
     ]
@@ -139,7 +141,7 @@
     ready = pltpu.get_barrier_semaphore()
     for step in places()[:-1]:
         pl.semaphore_signal(ready, inc=1, device_id=step, device_id_type=MESH)
-    for load in loads[:4]:
+    for load in loads[:7]:
         load.wait()
     ask[...] = jnp.zeros_like(ask)
     ask[0:4, 0:8] = near[...]
@@ -168,7 +170,7 @@
     send(2)
     send(3)
 
-    for load in loads[4:]:
+    for load in loads[7:]:
         load.wait()
 
     for pad in (pad1, pad2):
@@ -238,20 +240,25 @@
                 give_c[level, k - 4] = ends.astype(BF16)
 
     def halo_terms(level, w):
-        for k in range(4):
-            ends = get_c[level, k].astype(F32)
+        copies = halo_copies(level)
+        sums = [None] * 4
+        for side in (2, 3, 0, 1):
+            if side == 0:
+                for k in range(4):
+                    copies[k].wait_recv()
+                    ends = get_c[level, k].astype(F32)
+                    at_c = LEFT - 1 if k % 2 == 0 else LEFT + SIDE
+                    for j in range(TILES):
+                        lines[j, k // 2, at_c : at_c + 1] = ends[j : j + 1]
+            copies[4 + side].wait_recv()
+            taps = (w[0], w[2], w[:, 0], w[:, 2])[side].reshape(3 * CH, CH)
             for j in range(TILES):
-                lines[j, k, LEFT : LEFT + SIDE] = get[level, k, j].astype(F32)
-                at_c = LEFT - 1 if k % 2 == 0 else LEFT + SIDE
-                lines[j, k // 2, at_c : at_c + 1] = ends[j : j + 1]
-        sums = []
-        for side, taps in enumerate((w[0], w[2], w[:, 0], w[:, 2])):
-            for j in range(TILES):
+                lines[j, side, LEFT : LEFT + SIDE] = get[level, side, j].astype(F32)
                 for n in range(3):
                     beyond[side, j * SIDE : (j + 1) * SIDE, n * CH : (n + 1) * CH] = lines[
                         j, side, LEFT - 1 + n : LEFT - 1 + n + SIDE
                     ].astype(BF16)
-            sums.append(jnp.dot(beyond[side], taps.reshape(3 * CH, CH), preferred_element_type=F32))
+            sums[side] = jnp.dot(beyond[side], taps, preferred_element_type=F32)
         r = lax.broadcasted_iota(jnp.int32, (SIDE, CH), 0)
 
         def both_ends(v, first, last):
@@ -377,8 +384,6 @@
 
         @pl.when(j == TILES - 1)
         def _():
-            for h in halo_copies(0):
-                h.wait_recv()
             terms = halo_terms(0, w1)
             for i in range(TILES):
                 turn(1, i * 4, [gelu(part + term).astype(BF16) for part, term in zip(edges(i), terms[i])])
@@ -450,8 +455,6 @@
         return 0
 
     lax.fori_loop(0, TILES - 1, rings, 0)
-    for h in halo_copies(1):
-        h.wait_recv()
     terms = halo_terms(1, w2)
     for i in range(TILES):
         finish(i, 0, [part + term for part, term in zip(edges(i), terms[i])])
@@ -484,7 +487,7 @@
             pltpu.VMEM((1, CH), F32),
             pltpu.VMEM((3, 3, CH, CH), BF16),
             pltpu.VMEM((1, CH), F32),
-            dma((9,)),
+            dma((12,)),
             pltpu.VMEM((TILES, RANKS, BLOCK, CH), BF16),
             pltpu.VMEM((TILES, RANKS, BLOCK, CH), BF16),
             pltpu.VMEM((TILES, SIDE + 2, WIDE, CH), F32),

time: 76.6 us -> 76.9 us (level)
  no operation moved by 1% of the time
where the time goes in v5:
time: 76.9 us; the launch traced here: 76.8 us
  Pallas kernels  74.8 us (97%)
  local copies, waits for them, and re-layouts  2.02 us (3%)
    pallas_call x1, Pallas kernels, shards(): pl.pallas_call(kernel, out_shape=jax.ShapeDtypeStruct((TILES, SIDE, SIDE,...  74.8 us
    unnamed x1, local copies, waits for them, and re-layouts  2.02 us

profile of v5, /device:TPU:1, one launch (start us, length us, event | category | flops | bytes accessed | tf_op | source)
XLA Modules:
  0.0 76.8 jit_solution(3575134073743802193)
XLA Ops:
  0.0 74.8 %level.1 = bf16[4,64,64,128]{3,2,1,0:T(8,128)(2,1)S(1)} custom-call(s32[512]{0:T(512)} %order_h.1, s32[32]{0:T(128)} %constant.2.clone.table_h, bf16[512,32,128]{2,1,0:T(8,128)(2,1)} %lat_h.1, s32[4,8]{1,0:T(4,128)} %near_h.1, s32[4,8]{1,0:T(4,128)} %turns_h.1, bf16[3,3,128,128]{3,2,1,0:T(8,128)(2,1)} %w1_h.1, f32[1,128]{1,0:T(1,128)} %bitcast.2, ...), custom_call_target="tpu_custom_call" | custom-call | tf_op jit(solution)/shard_map/level/pallas_call | solution.py:475
  74.8 2.0 %copy.11 = bf16[4,64,64,128]{3,2,1,0:T(8,128)(2,1)} copy(bf16[4,64,64,128]{3,2,1,0:T(8,128)(2,1)S(1)} %level.1) | data formatting | bytes 8388608
